TPU v7x, 256 devices: a whole 4x4x8 slice. The times are simulated.
256 devices in a mesh: rep: 2 (over z_hi), fsdp: 32 (over y, x, core), tp: 4 (over z_lo).
Axes of the slice: x: 4, y: 4, z: 8 (z_hi: 2, z_lo: 4; z = z_hi * 4 + z_lo), core: 2. Of those that a mesh axis runs over, the one named last changes fastest.
Arguments:
- delta_out: float32 [2, 8, 1792, 1792], P('rep', None, 'tp', 'fsdp'), may hold values from -6 to 6
- delta_down: float32 [2, 8, 4864, 1792], P('rep', None, 'tp', 'fsdp'), may hold values from -6 to 6
- basis: float32 [1792, 64], replicated, may hold values from -0.125 to 0.125
- anchor_out: float32 [8, 4, 448, 1792], P('rep', 'tp', 'fsdp'), may hold values from -6 to 6
- anchor_down: float32 [8, 4, 1216, 1792], P('rep', 'tp', 'fsdp'), may hold values from -6 to 6
- moment_out: float32 [8, 4, 448, 1792], P('rep', 'tp', 'fsdp'), may hold values from -3 to 3
- moment_down: float32 [8, 4, 1216, 1792], P('rep', 'tp', 'fsdp'), may hold values from -3 to 3
Outputs:
- weights_out: bfloat16 [8, 1792, 1792], P(None, 'tp', 'fsdp')
- weights_down: bfloat16 [8, 4864, 1792], P(None, 'tp', 'fsdp')
- anchor_out_new: float32 [8, 4, 448, 1792], P('rep', 'tp', 'fsdp')
- anchor_down_new: float32 [8, 4, 1216, 1792], P('rep', 'tp', 'fsdp')
- moment_out_new: float32 [8, 4, 448, 1792], P('rep', 'tp', 'fsdp')
- moment_down_new: float32 [8, 4, 1216, 1792], P('rep', 'tp', 'fsdp')
All inputs are finite; a program needn't handle non-finite values.
Results may differ from a plain program's by a relative error of at most 0.0055.
Values may be sent and summed in bfloat16 or wider, within the bound.
A program may use at most 64 MiB of HBM per device.

v0:
```python
import jax
import jax.numpy as jnp
from jax import lax
from jax.sharding import PartitionSpec as P

outer_rate = 0.7
nesterov_decay = 0.9


def owner_update(summed, basis, anchor, moment, groups):
    coef = summed / groups
    grad = jnp.einsum("lik,jk->lij", coef, basis, precision=lax.Precision.HIGHEST)
    previous = anchor[:, 0]
    velocity = moment[:, 0]
    moment_new = nesterov_decay * velocity + grad
    anchor_new = previous - outer_rate * (grad + nesterov_decay * moment_new)
    return (anchor_new, moment_new)


def per_device(delta_out, delta_down, basis, anchor_out, anchor_down, moment_out, moment_down):
    groups = lax.axis_size("rep")
    piece_cols = delta_out.shape[3]
    shard_index = lax.axis_index("fsdp")
    basis_rows = lax.dynamic_slice_in_dim(basis, shard_index * piece_cols, piece_cols, 0)
    partial_out = jnp.einsum(
        "lij,jk->lik", delta_out[0], basis_rows, precision=lax.Precision.HIGHEST
    )
    partial_down = jnp.einsum(
        "lij,jk->lik", delta_down[0], basis_rows, precision=lax.Precision.HIGHEST
    )
    layer_sums = (
        lax.psum_scatter(
            partial_out.astype(jnp.bfloat16), "rep", scatter_dimension=0, tiled=True
        ).astype(jnp.float32),
        lax.psum_scatter(
            partial_down.astype(jnp.bfloat16), "rep", scatter_dimension=0, tiled=True
        ).astype(jnp.float32),
    )
    summed_out, summed_down = (
        lax.psum_scatter(
            layer_sums[0].astype(jnp.bfloat16), "fsdp", scatter_dimension=1, tiled=True
        ).astype(jnp.float32),
        lax.psum_scatter(
            layer_sums[1].astype(jnp.bfloat16), "fsdp", scatter_dimension=1, tiled=True
        ).astype(jnp.float32),
    )
    anchor_out_new, moment_out_new = owner_update(summed_out, basis, anchor_out, moment_out, groups)
    anchor_down_new, moment_down_new = owner_update(
        summed_down, basis, anchor_down, moment_down, groups
    )
    rounded_out = anchor_out_new.astype(jnp.bfloat16)
    rounded_down = anchor_down_new.astype(jnp.bfloat16)
    placed_out, placed_down = (
        lax.all_to_all(rounded_out, "fsdp", split_axis=2, concat_axis=1, tiled=True),
        lax.all_to_all(rounded_down, "fsdp", split_axis=2, concat_axis=1, tiled=True),
    )
    weights_out, weights_down = (
        lax.all_gather(placed_out, "rep", axis=0, tiled=True),
        lax.all_gather(placed_down, "rep", axis=0, tiled=True),
    )
    return (
        weights_out,
        weights_down,
        anchor_out_new[:, None],
        anchor_down_new[:, None],
        moment_out_new[:, None],
        moment_down_new[:, None],
    )


def solution(mesh):
    return jax.shard_map(
        per_device,
        mesh=mesh,
        in_specs=(
            P("rep", None, "tp", "fsdp"),
            P("rep", None, "tp", "fsdp"),
            P(),
            P("rep", "tp", "fsdp", None),
            P("rep", "tp", "fsdp", None),
            P("rep", "tp", "fsdp", None),
            P("rep", "tp", "fsdp", None),
        ),
        out_specs=(
            P(None, "tp", "fsdp"),
            P(None, "tp", "fsdp"),
            P("rep", "tp", "fsdp", None),
            P("rep", "tp", "fsdp", None),
            P("rep", "tp", "fsdp", None),
            P("rep", "tp", "fsdp", None),
        ),
        check_vma=False,
    )
```

profile of v0, /device:TPU:32, one launch (start us, length us, event | category | flops | bytes accessed | tf_op | source)
XLA Modules:
  0.0 316.6 jit_solution(11942777162929042482)
XLA Ops:
  7.2 0.0 copy-start
  7.2 0.0 reduce-scatter.3.cloned.1.call-start
  7.2 3.2 %fusion.2 = bf16[8,448,64]{1,2,0:T(8,128)(2,1)} fusion(f32[1,8,448,56]{2,3,1,0:T(8,128)} %param.7, f32[1792,64]{0,1:T(8,128)} %param.9, s32[]{:T(128)S(6)} %select_n.3), kind=kOutput, calls=%fused_computation.5 | convolution fusion | flops 154370048 | bytes 1409028 | tf_op jit(solution)/shard_map/lij,jk->lik/dot_general | solution.py:25
  10.4 0.0 reduce-scatter.3.cloned.1.call-update
  10.4 0.0 reduce-scatter.5.cloned.1.call-start
  10.5 0.0 copy-done
  10.5 4.2 %fusion = bf16[8,1216,64]{1,2,0:T(8,128)(2,1)} fusion(f32[1,8,1216,56]{2,3,1,0:T(8,128)S(1)} %copy-done, f32[1792,64]{0,1:T(8,128)} %param.9, s32[]{:T(128)S(6)} %select_n.3), kind=kOutput, calls=%fused_computation.1 | convolution fusion | flops 419004416 | bytes 3457028 | tf_op jit(solution)/shard_map/lij,jk->lik/dot_general | solution.py:28
  14.7 0.0 reduce-scatter.5.cloned.1.call-update
  14.7 0.0 all-reduce.5.cloned.1.call-start
  14.8 27.6 %reduce-scatter.3.cloned.1.call-done = bf16[4,448,64]{1,2,0:T(8,128)(2,1)} async-done(((bf16[8,448,64]{1,2,0:T(8,128)(2,1)}), bf16[4,448,64]{1,2,0:T(8,128)(2,1)}) %reduce-scatter.3.cloned.1.call-update) | async-done | bytes 229392 | tf_op jit(solution)/shard_map/reduce_scatter | solution.py:32
  42.3 2.0 copy.35
  44.3 43.5 %reduce-scatter.5.cloned.1.call-done = bf16[4,1216,64]{1,2,0:T(8,128)(2,1)} async-done(((bf16[8,1216,64]{1,2,0:T(8,128)(2,1)}), bf16[4,1216,64]{1,2,0:T(8,128)(2,1)}) %reduce-scatter.5.cloned.1.call-update) | async-done | bytes 622608 | tf_op jit(solution)/shard_map/reduce_scatter | solution.py:35
  87.8 3.2 %copy.43 = bf16[4,1216,64]{2,0,1:T(4,128)(2,1)} copy(bf16[4,1216,64]{1,2,0:T(8,128)(2,1)} %reduce-scatter.5.cloned.1.call-done) | data formatting | bytes 1245184 | tf_op jit(solution)/shard_map/reduce_scatter | solution.py:35
  91.0 0.0 copy-start.4
  91.0 0.0 all-reduce.5.cloned.1.call-update
  91.1 0.0 all-gather.2.cloned.1.call-start
  91.1 0.6 copy-done.4
  91.7 0.6 dynamic-slice
  93.0 112.2 %all-reduce.5.cloned.1.call-done = (bf16[4,448,64]{2,0,1:T(4,128)(2,1)}, bf16[4,1216,64]{2,0,1:T(4,128)(2,1)}) async-done(((bf16[4,448,64]{2,0,1:T(4,128)(2,1)}, bf16[4,1216,64]{2,0,1:T(4,128)(2,1)}), (bf16[4,448,64]{2,0,1:T(4,128)(2,1)}, bf16[4,1216,64]{2,0,1:T(4,128)(2,1)})) %all-reduce.5.cloned.1.call-update) | async-done | bytes 851984
  205.2 0.8 convert_multiply_fusion
  205.9 4.2 %fusion.20 = (f32[4,1,38,1792]{3,2,0,1:T(8,128)}, bf16[4,38,1792]{2,1,0:T(8,128)(2,1)}, f32[4,1,38,1792]{3,2,0,1:T(8,128)S(1)}) fusion(f32[4,1,38,1792]{3,1,2,0:T(1,128)} %param.13, f32[4,1,38,1792]{3,1,2,0:T(1,128)} %param.11, f32[1792,64]{0,1:T(8,128)} %param.9, f32[4,38,64]{2,0,1:T(4,128)S(1)} %convert_multiply_fusion), kind=kOutput, calls=%fused_computation.32 | convolution fusion | flops 211097600 | bytes 5400576 | tf_op jit(solution)/shard_map/lik,jk->lij/dot_general | solution.py:12
  210.1 3.6 %copy.46 = bf16[4,38,1792]{1,0,2:T(4,128)(2,1)} copy(bf16[4,38,1792]{2,1,0:T(8,128)(2,1)} %get-tuple-element.27) | data formatting | bytes 1089536 | tf_op jit(solution)/shard_map/convert_element_type | solution.py:52
  213.7 5.8 %reshape.22 = bf16[32,2,4256]{2,1,0:T(2,128)(2,1)} reshape(bf16[1792,4,38]{2,1,0:T(4,128)(2,1)} %bitcast.82) | data formatting | bytes 1089536
  219.4 17.7 %all_to_all.36 = bf16[32,2,4256]{2,1,0:T(2,128)(2,1)} all-to-all(bf16[32,2,4256]{2,1,0:T(2,128)(2,1)} %reshape.22), channel_id=1, replica_groups=mesh['rep'=2,'fsdp'=32,'tp'=4] {'fsdp'}, dimensions={0} | all-to-all | bytes 1089536 | tf_op jit(solution)/shard_map/all_to_all | solution.py:55
  237.2 7.4 %reshape.23 = bf16[1792,4,38]{2,1,0:T(4,128)(2,1)} reshape(bf16[32,2,4256]{2,1,0:T(2,128)(2,1)} %all_to_all.36) | data formatting | bytes 1089536
  244.6 3.5 %copy.100 = bf16[4,38,32,56]{1,2,3,0:T(8,128)(2,1)} copy(bf16[4,38,32,56]{1,0,3,2:T(4,128)(2,1)} %bitcast.80) | data formatting | bytes 1089536 | tf_op jit(solution)/shard_map/all_to_all | solution.py:55
  248.0 4.7 %all_to_all.33 = bf16[4,1216,56]{1,2,0:T(8,128)(2,1)} reshape(bf16[4,32,38,56]{2,1,3,0:T(8,128)(2,1)} %bitcast.81) | data formatting | bytes 1089536 | tf_op jit(solution)/shard_map/all_to_all | solution.py:55
  252.7 0.0 all-gather.2.cloned.1.call-update
  253.4 0.0 copy-start.1
  253.4 1.2 copy.101
  254.5 0.7 convert_multiply_fusion.1
  255.3 0.0 copy-done.1
  255.3 2.6 fusion.18
  257.9 3.3 %copy.39 = bf16[4,14,1792]{1,0,2:T(4,128)(2,1)} copy(bf16[4,14,1792]{2,1,0:T(8,128)(2,1)} %get-tuple-element.30) | data formatting | bytes 401408 | tf_op jit(solution)/shard_map/convert_element_type | solution.py:51
  261.2 4.8 %reshape.20 = bf16[32,2,1568]{2,1,0:T(2,128)(2,1)} reshape(bf16[1792,4,14]{2,1,0:T(4,128)(2,1)} %bitcast.83) | data formatting | bytes 401408
  266.1 4.8 %all-to-all-start = ((bf16[32,2,1568]{2,1,0:T(2,128)(2,1)}), bf16[32,2,1568]{2,1,0:T(2,128)(2,1)}, u32[]{:S(2)}, u32[]{:S(2)}) async-start(bf16[32,2,1568]{2,1,0:T(2,128)(2,1)} %reshape.20), calls=%async_computation.1 | async-start | bytes 425984 | tf_op jit(solution)/shard_map/all_to_all | solution.py:54
  270.8 3.4 %copy.50 = f32[4,1,38,1792]{3,1,2,0:T(1,128)} copy(f32[4,1,38,1792]{3,2,0,1:T(8,128)} %get-tuple-element.26) | data formatting | bytes 2179072
  274.2 0.0 copy-start.3
  274.2 0.0 copy-start.2
  274.2 2.1 copy.52
  276.3 0.0 copy-done.3
  276.3 1.2 copy.49
  277.5 0.0 copy-done.2
  277.5 1.2 copy.51
  278.7 0.3 all-to-all-done
  279.0 6.8 %reshape.21 = bf16[1792,4,14]{2,1,0:T(4,128)(2,1)} reshape(bf16[32,2,1568]{2,1,0:T(2,128)(2,1)} %all-to-all-done) | data formatting | bytes 401408
  285.8 3.4 %copy.53 = bf16[4,14,32,56]{3,2,0,1:T(8,128)(2,1)S(1)} copy(bf16[4,14,32,56]{1,0,3,2:T(4,128)(2,1)} %bitcast.84) | data formatting | bytes 401408 | tf_op jit(solution)/shard_map/all_to_all | solution.py:54
  289.1 0.2 copy.41
  289.4 0.3 copy.42
  289.7 17.3 %all_gather.6 = bf16[8,448,56]{1,2,0:T(8,128)(2,1)S(1)} all-gather(bf16[4,448,56]{1,2,0:T(8,128)(2,1)S(1)} %copy.42), channel_id=1, replica_groups=mesh['rep'=2,'fsdp'=32,'tp'=4] {'rep'}, dimensions={0}, use_global_device_ids=true | all-gather | bytes 602112 | tf_op jit(solution)/shard_map/all_gather | solution.py:58
  307.0 0.0 all-gather.2.cloned.1.call-done
  307.0 0.8 copy.106
  307.8 2.3 copy.107
Async XLA Ops:
  7.2 3.3 %copy-start = (f32[1,8,1216,56]{2,3,1,0:T(8,128)S(1)}, f32[1,8,1216,56]{2,3,1,0:T(8,128)}, u32[]{:S(2)}) copy-start(f32[1,8,1216,56]{2,3,1,0:T(8,128)} %param.8) | copy-start | bytes 6537220
  7.2 35.2 %reduce-scatter.3.cloned.1.call-start = ((), (), s32[]{:S(2)}) async-start(), calls=%async_computation.4 | async-start | bytes 786432 | tf_op jit(solution)/shard_map/reduce_scatter | solution.py:32
  10.4 77.4 %reduce-scatter.5.cloned.1.call-start = ((), (), s32[]{:S(2)}) async-start(), calls=%async_computation.5 | async-start | bytes 1966080 | tf_op jit(solution)/shard_map/reduce_scatter | solution.py:35
  14.7 190.4 %all-reduce.5.cloned.1.call-start = ((), (), s32[]{:S(2)}) async-start(), calls=%async_computation.7 | async-start | bytes 3407872
  91.0 0.7 copy-start.4
  91.1 215.9 %all-gather.2.cloned.1.call-start = ((), (), s32[]{:S(2)}) async-start(), calls=%async_computation.6 | async-start | bytes 1720320 | tf_op jit(solution)/shard_map/all_gather | solution.py:59
  253.4 1.9 copy-start.1
  266.1 12.9 %all-to-all-start = ((bf16[32,2,1568]{2,1,0:T(2,128)(2,1)}), bf16[32,2,1568]{2,1,0:T(2,128)(2,1)}, u32[]{:S(2)}, u32[]{:S(2)}) async-start(bf16[32,2,1568]{2,1,0:T(2,128)(2,1)} %reshape.20), calls=%async_computation.1 | async-start | bytes 425984 | tf_op jit(solution)/shard_map/all_to_all | solution.py:54
  274.2 2.1 copy-start.3
  274.2 3.3 %copy-start.2 = (f32[4,1,14,1792]{3,2,0,1:T(8,128)S(1)}, f32[4,1,14,1792]{3,2,0,1:T(8,128)}, u32[]{:S(2)}) copy-start(f32[4,1,14,1792]{3,2,0,1:T(8,128)} %get-tuple-element.31) | copy-start | bytes 1204228
Sparse Core Ops, SparseCore 0:
  11.1 31.2 reduce-scatter.2
  45.0 42.7 reduce-scatter.4
  91.8 113.3 all-reduce.4
  252.8 40.9 all-gather.1
where the time goes:
time: 318 us; the launch traced here: 317 us
  waiting for transfers between devices  184 us (58%)
  local copies, waits for them, and re-layouts  62.2 us (20%)
  blocking collectives  35 us (11%)
  between operations  15.2 us (5%)
  matrix products  14.1 us (4%)
  starting transfers between devices  4.95 us (2%)
    unnamed x5, waiting for transfers between devices  112 us
    reduce_scatter x1, waiting for transfers between devices, per_device(): lax.psum_scatter(partial_down.astype(jnp.bfloat16), 'rep', scatter_dimens...  43.5 us
    unnamed x22, local copies, waits for them, and re-layouts  38 us
    reduce_scatter x1, waiting for transfers between devices, per_device(): lax.psum_scatter(partial_out.astype(jnp.bfloat16), 'rep', scatter_dimensi...  27.6 us
    all_to_all x1, blocking collectives, per_device(): lax.all_to_all(rounded_down, 'fsdp', split_axis=2, concat_axis=1, tiled=T...  17.7 us
    all_gather x1, blocking collectives, per_device(): lax.all_gather(placed_out, 'rep', axis=0, tiled=True)  17.3 us
    all_to_all x2, local copies, waits for them, and re-layouts, per_device(): lax.all_to_all(rounded_down, 'fsdp', split_axis=2, concat_axis=1, tiled=T...  8.1 us
    dot_general x2, matrix products, owner_update(): jnp.einsum('lik,jk->lij', coef, basis, precision=lax.Precision.HIGHEST)  6.77 us
  transfers between devices with their start and end apart: 5, of which 4 were waited for; matrix products, arithmetic and copies ran while one was open for 12% of the time, Pallas kernels for 0%

commit v1 on v0

--- a/solution.py
+++ b/solution.py
@@ -52,7 +52,12 @@
     rounded_down = anchor_down_new.astype(jnp.bfloat16)
     placed_out, placed_down = (
         lax.all_to_all(rounded_out, "fsdp", split_axis=2, concat_axis=1, tiled=True),
-        lax.all_to_all(rounded_down, "fsdp", split_axis=2, concat_axis=1, tiled=True),
+        jnp.concatenate(
+            lax.all_to_all(
+                jnp.stack(jnp.split(rounded_down, lax.axis_size("fsdp"), axis=2)), "fsdp", 0, 0
+            ),
+            axis=1,
+        ),
     )
     weights_out, weights_down = (
         lax.all_gather(placed_out, "rep", axis=0, tiled=True),

time: 318 us -> 303 us (0.953)
  local copies, waits for them, and re-layouts: 62.2 us -> 48.9 us
    all_to_all x2 -> x0, local copies, waits for them, and re-layouts: 8.1 us -> none  [per_device(): lax.all_to_all(rounded_down, 'fsdp', split_axis=2, concat_axis=1, tiled=T...]
    unnamed x22 -> x57, local copies, waits for them, and re-layouts: 38 us -> 34.5 us
    convert_element_type x1 -> x0, local copies, waits for them, and re-layouts: 3.56 us -> none  [per_device(): rounded_down = anchor_down_new.astype(jnp.bfloat16)]
  transfers between devices with their start and end apart: 5 -> 5, of which waited for: 4 -> 3; matrix products, arithmetic and copies ran while one was open for 12% -> 12% of each run, Pallas kernels for 0% -> 0%
where the time goes in v1:
time: 303 us; the launch traced here: 302 us
  waiting for transfers between devices  184 us (61%)
  local copies, waits for them, and re-layouts  48.9 us (16%)
  blocking collectives  34.6 us (11%)
  between operations  15.4 us (5%)
  matrix products  12.3 us (4%)
  starting transfers between devices  5.09 us (2%)
    unnamed x5, waiting for transfers between devices  112 us
    reduce_scatter x1, waiting for transfers between devices, per_device(): lax.psum_scatter(partial_down.astype(jnp.bfloat16), 'rep', scatter_dimens...  43.5 us
    unnamed x57, local copies, waits for them, and re-layouts  34.5 us
    reduce_scatter x1, waiting for transfers between devices, per_device(): lax.psum_scatter(partial_out.astype(jnp.bfloat16), 'rep', scatter_dimensi...  28.4 us
    all_to_all x1, blocking collectives, per_device(): lax.all_to_all(jnp.stack(jnp.split(rounded_down, lax.axis_size('fsdp'), a...  17.7 us
    all_gather x1, blocking collectives, per_device(): lax.all_gather(placed_out, 'rep', axis=0, tiled=True)  16.9 us
  transfers between devices with their start and end apart: 5, of which 3 were waited for; matrix products, arithmetic and copies ran while one was open for 12% of the time, Pallas kernels for 0%

profile of v1, /device:TPU:32, one launch (start us, length us, event | category | flops | bytes accessed | tf_op | source)
XLA Modules:
  0.0 302.0 jit_solution(9035037345845403970)
XLA Ops:
  7.2 3.2 %fusion.2 = bf16[8,448,64]{1,2,0:T(8,128)(2,1)} fusion(f32[1,8,448,56]{2,3,1,0:T(8,128)} %param.7, f32[1792,64]{0,1:T(8,128)} %param.9, s32[]{:T(128)S(6)} %select_n.3), kind=kOutput, calls=%fused_computation.4 | convolution fusion | flops 154370048 | bytes 1409028 | tf_op jit(solution)/shard_map/lij,jk->lik/dot_general | solution.py:25
  10.5 3.3 %fusion = bf16[8,1216,64]{1,2,0:T(8,128)(2,1)} fusion(f32[1,8,1216,56]{2,3,1,0:T(8,128)S(1)} %copy-done, f32[1792,64]{0,1:T(8,128)S(1)} %copy-done.3, s32[]{:T(128)S(6)} %select_n.3), kind=kOutput, calls=%fused_computation.1 | convolution fusion | flops 419004416 | bytes 3571716 | tf_op jit(solution)/shard_map/lij,jk->lik/dot_general | solution.py:28
  13.9 28.4 %reduce-scatter.3.cloned.1.call-done = bf16[4,448,64]{1,2,0:T(8,128)(2,1)} async-done(((bf16[8,448,64]{1,2,0:T(8,128)(2,1)}), bf16[4,448,64]{1,2,0:T(8,128)(2,1)}) %reduce-scatter.3.cloned.1.call-update) | async-done | bytes 229392 | tf_op jit(solution)/shard_map/reduce_scatter | solution.py:32
  42.3 2.0 copy.34
  44.3 43.5 %reduce-scatter.5.cloned.1.call-done = bf16[4,1216,64]{1,2,0:T(8,128)(2,1)} async-done(((bf16[8,1216,64]{1,2,0:T(8,128)(2,1)}), bf16[4,1216,64]{1,2,0:T(8,128)(2,1)}) %reduce-scatter.5.cloned.1.call-update) | async-done | bytes 622608 | tf_op jit(solution)/shard_map/reduce_scatter | solution.py:35
  87.8 3.2 %copy.42 = bf16[4,1216,64]{2,0,1:T(4,128)(2,1)} copy(bf16[4,1216,64]{1,2,0:T(8,128)(2,1)} %reduce-scatter.5.cloned.1.call-done) | data formatting | bytes 1245184 | tf_op jit(solution)/shard_map/reduce_scatter | solution.py:35
  91.1 0.0 all-gather.2.cloned.1.call-start
  91.1 0.6 copy-done.6
  91.7 0.6 dynamic-slice
  93.0 112.2 %all-reduce.5.cloned.1.call-done = (bf16[4,448,64]{2,0,1:T(4,128)(2,1)}, bf16[4,1216,64]{2,0,1:T(4,128)(2,1)}) async-done(((bf16[4,448,64]{2,0,1:T(4,128)(2,1)}, bf16[4,1216,64]{2,0,1:T(4,128)(2,1)}), (bf16[4,448,64]{2,0,1:T(4,128)(2,1)}, bf16[4,1216,64]{2,0,1:T(4,128)(2,1)})) %all-reduce.5.cloned.1.call-update) | async-done | bytes 851984
  205.2 0.8 convert_multiply_fusion
  206.0 4.2 %fusion.20 = (f32[4,1,38,1792]{3,2,0,1:T(8,128)}, bf16[4,38,1792]{2,1,0:T(8,128)(2,1)S(1)}, f32[4,1,38,1792]{3,2,0,1:T(8,128)}) fusion(f32[4,1,38,1792]{3,1,2,0:T(1,128)} %param.13, f32[4,1,38,1792]{3,1,2,0:T(1,128)} %param.11, f32[1792,64]{0,1:T(8,128)S(1)} %copy-done.3, f32[4,38,64]{2,0,1:T(4,128)S(1)} %convert_multiply_fusion), kind=kOutput, calls=%fused_computation.95 | convolution fusion | flops 211097600 | bytes 5400576 | tf_op jit(solution)/shard_map/lik,jk->lij/dot_general | solution.py:12
  210.2 0.1 constant_dynamic-update-slice_fusion.30
  210.3 0.1 constant_dynamic-update-slice_fusion.29
  210.4 0.1 constant_dynamic-update-slice_fusion.28
  210.5 0.1 constant_dynamic-update-slice_fusion.27
  210.6 0.1 constant_dynamic-update-slice_fusion.26
  210.7 0.1 constant_dynamic-update-slice_fusion.25
  210.7 0.1 constant_dynamic-update-slice_fusion.24
  210.8 0.1 constant_dynamic-update-slice_fusion.23
  210.9 0.1 constant_dynamic-update-slice_fusion.22
  211.0 0.1 constant_dynamic-update-slice_fusion.21
  211.1 0.1 constant_dynamic-update-slice_fusion.20
  211.2 0.1 constant_dynamic-update-slice_fusion.19
  211.3 0.1 constant_dynamic-update-slice_fusion.18
  211.4 0.1 constant_dynamic-update-slice_fusion.17
  211.5 0.1 constant_dynamic-update-slice_fusion.16
  211.6 0.1 constant_dynamic-update-slice_fusion.14
  211.7 0.1 constant_dynamic-update-slice_fusion.13
  211.8 0.1 constant_dynamic-update-slice_fusion.12
  211.9 0.1 constant_dynamic-update-slice_fusion.11
  212.0 0.1 constant_dynamic-update-slice_fusion.10
  212.1 0.1 constant_dynamic-update-slice_fusion.9
  212.2 0.1 constant_dynamic-update-slice_fusion.8
  212.3 0.1 constant_dynamic-update-slice_fusion.7
  212.4 0.1 constant_dynamic-update-slice_fusion.6
  212.5 0.1 constant_dynamic-update-slice_fusion.5
  212.6 0.1 constant_dynamic-update-slice_fusion.4
  212.7 0.1 constant_dynamic-update-slice_fusion.3
  212.8 0.1 constant_dynamic-update-slice_fusion.2
  212.9 0.1 constant_dynamic-update-slice_fusion.1
  213.0 0.1 constant_dynamic-update-slice_fusion
  213.1 0.5 copy.98
  213.5 2.8 reshape.30
  216.4 17.7 %all_to_all.23 = bf16[32,2,4256]{2,1,0:T(2,128)(2,1)} all-to-all(bf16[32,2,4256]{2,1,0:T(2,128)(2,1)} %reshape.30), channel_id=1, replica_groups=mesh['rep'=2,'fsdp'=32,'tp'=4] {'fsdp'}, dimensions={0} | all-to-all | bytes 1089536 | tf_op jit(solution)/shard_map/all_to_all | solution.py:56
  234.1 3.5 %reshape.31 = bf16[32,38,4,56]{3,2,1,0:T(4,128)(2,1)S(1)} reshape(bf16[32,2,4256]{2,1,0:T(2,128)(2,1)} %all_to_all.23) | data formatting | bytes 1089536
  237.6 2.4 copy.52
  240.7 1.1 copy.97
  241.8 0.7 convert_multiply_fusion.1
  242.6 1.6 fusion.18
  244.1 2.4 copy.38
  246.5 4.8 %reshape.28 = bf16[32,2,1568]{2,1,0:T(2,128)(2,1)} reshape(bf16[1792,4,14]{2,1,0:T(4,128)(2,1)} %bitcast.204) | data formatting | bytes 401408
  251.3 4.9 %all-to-all-start = ((bf16[32,2,1568]{2,1,0:T(2,128)(2,1)}), bf16[32,2,1568]{2,1,0:T(2,128)(2,1)}, u32[]{:S(2)}, u32[]{:S(2)}) async-start(bf16[32,2,1568]{2,1,0:T(2,128)(2,1)} %reshape.28), calls=%async_computation.1 | async-start | bytes 425984 | tf_op jit(solution)/shard_map/all_to_all | solution.py:54
  256.2 2.2 copy.47
  258.4 2.2 copy.49
  260.6 2.1 copy.48
  262.7 2.1 copy.50
  264.8 6.7 %reshape.29 = bf16[1792,4,14]{2,1,0:T(4,128)(2,1)} reshape(bf16[32,2,1568]{2,1,0:T(2,128)(2,1)} %all-to-all-done) | data formatting | bytes 401408
  271.5 3.4 %copy.51 = bf16[4,14,32,56]{3,2,0,1:T(8,128)(2,1)S(1)} copy(bf16[4,14,32,56]{1,0,3,2:T(4,128)(2,1)} %bitcast.205) | data formatting | bytes 401408 | tf_op jit(solution)/shard_map/all_to_all | solution.py:54
  274.9 0.2 copy.40
  275.1 0.3 copy.41
  275.4 16.9 %all_gather.6 = bf16[8,448,56]{1,2,0:T(8,128)(2,1)S(1)} all-gather(bf16[4,448,56]{1,2,0:T(8,128)(2,1)S(1)} %copy.41), channel_id=1, replica_groups=mesh['rep'=2,'fsdp'=32,'tp'=4] {'rep'}, dimensions={0}, use_global_device_ids=true | all-gather | bytes 602112 | tf_op jit(solution)/shard_map/all_gather | solution.py:63
  292.3 0.8 copy.134
  293.1 2.3 copy.135
  (24 shorter events, 0.2 us)
Async XLA Ops:
  7.2 3.3 %copy-start = (f32[1,8,1216,56]{2,3,1,0:T(8,128)S(1)}, f32[1,8,1216,56]{2,3,1,0:T(8,128)}, u32[]{:S(2)}) copy-start(f32[1,8,1216,56]{2,3,1,0:T(8,128)} %param.8) | copy-start | bytes 6537220
  7.2 3.3 %copy-start.3 = (f32[1792,64]{0,1:T(8,128)S(1)}, f32[1792,64]{0,1:T(8,128)}, u32[]{:S(2)}) copy-start(f32[1792,64]{0,1:T(8,128)} %param.9) | copy-start | bytes 1376260
  7.2 35.2 %reduce-scatter.3.cloned.1.call-start = ((), (), s32[]{:S(2)}) async-start(), calls=%async_computation.4 | async-start | bytes 786432 | tf_op jit(solution)/shard_map/reduce_scatter | solution.py:32
  10.5 77.4 %reduce-scatter.5.cloned.1.call-start = ((), (), s32[]{:S(2)}) async-start(), calls=%async_computation.5 | async-start | bytes 1966080 | tf_op jit(solution)/shard_map/reduce_scatter | solution.py:35
  13.9 191.3 %all-reduce.5.cloned.1.call-start = ((), (), s32[]{:S(2)}) async-start(), calls=%async_computation.7 | async-start | bytes 3407872
  91.1 0.7 copy-start.6
  91.1 201.2 %all-gather.2.cloned.1.call-start = ((), (), s32[]{:S(2)}) async-start(), calls=%async_computation.6 | async-start | bytes 1720320 | tf_op jit(solution)/shard_map/all_gather | solution.py:64
  240.0 2.6 copy-start.4
  240.0 2.6 copy-start.5
  251.3 9.3 %copy-start.2 = (f32[4,1,38,1792]{3,2,0,1:T(8,128)S(1)}, f32[4,1,38,1792]{3,2,0,1:T(8,128)}, u32[]{:S(2)}) copy-start(f32[4,1,38,1792]{3,2,0,1:T(8,128)} %get-tuple-element.26) | copy-start | bytes 3268612
  251.3 13.5 %all-to-all-start = ((bf16[32,2,1568]{2,1,0:T(2,128)(2,1)}), bf16[32,2,1568]{2,1,0:T(2,128)(2,1)}, u32[]{:S(2)}, u32[]{:S(2)}) async-start(bf16[32,2,1568]{2,1,0:T(2,128)(2,1)} %reshape.28), calls=%async_computation.1 | async-start | bytes 425984 | tf_op jit(solution)/shard_map/all_to_all | solution.py:54
  260.6 2.1 copy-start.1
Sparse Core Ops, SparseCore 0:
  11.1 31.2 reduce-scatter.2
  45.0 42.7 reduce-scatter.4
  91.8 113.3 all-reduce.4
  240.1 40.9 all-gather.1
